TPU v7x, 32 devices: a whole 2x2x4 slice. The times are simulated.
32 devices in a mesh: dp: 16 (over z, y, core), tensor: 2 (over x).
Axes of the slice: x: 2, y: 2, z: 4, core: 2. Of those that a mesh axis runs over, the one named last changes fastest.
Arguments:
- tokens: bfloat16 [32, 448, 1024], P('dp'), may hold values from -6 to 6
- encoded: bfloat16 [32, 1500, 1024], P('dp'), may hold values from -6 to 6
- cotangent: bfloat16 [32, 448, 1024], P('dp'), may hold values from -6 to 6
- self_gain: bfloat16 [1024], replicated, may hold values from 0.5 to 1.5
- self_shift: bfloat16 [1024], replicated, may hold values from -1.75 to 1.75
- self_query: bfloat16 [1024, 1024], P(None, 'tensor'), may hold values from -0.25 to 0.25
- self_query_bias: bfloat16 [1024], P('tensor'), may hold values from -1.75 to 1.75
- self_key: bfloat16 [1024, 1024], P(None, 'tensor'), may hold values from -0.1875 to 0.1875
- self_value: bfloat16 [1024, 1024], P(None, 'tensor'), may hold values from -0.1875 to 0.1875
- self_value_bias: bfloat16 [1024], P('tensor'), may hold values from -1.75 to 1.75
- self_mixer: bfloat16 [1024, 1024], P('tensor'), may hold values from -0.5 to 0.5
- self_mixer_bias: bfloat16 [1024], replicated, may hold values from -1.75 to 1.75
- cross_gain: bfloat16 [1024], replicated, may hold values from 0.5 to 1.5
- cross_shift: bfloat16 [1024], replicated, may hold values from -1.75 to 1.75
- cross_query: bfloat16 [1024, 1024], P(None, 'tensor'), may hold values from -0.25 to 0.25
- cross_query_bias: bfloat16 [1024], P('tensor'), may hold values from -1.75 to 1.75
- cross_key: bfloat16 [1024, 1024], P(None, 'tensor'), may hold values from -0.1875 to 0.1875
- cross_value: bfloat16 [1024, 1024], P(None, 'tensor'), may hold values from -0.1875 to 0.1875
- cross_value_bias: bfloat16 [1024], P('tensor'), may hold values from -1.75 to 1.75
- cross_mixer: bfloat16 [1024, 1024], P('tensor'), may hold values from -0.75 to 0.75
- cross_mixer_bias: bfloat16 [1024], replicated, may hold values from -1.75 to 1.75
- feed_gain: bfloat16 [1024], replicated, may hold values from 0.5 to 1.5
- feed_shift: bfloat16 [1024], replicated, may hold values from -1.75 to 1.75
- expand_weight: bfloat16 [1024, 4096], P(None, 'tensor'), may hold values from -0.1875 to 0.1875
- expand_bias: bfloat16 [4096], P('tensor'), may hold values from -3 to 3
- reduce_weight: bfloat16 [4096, 1024], P('tensor'), may hold values from -0.125 to 0.125
- reduce_bias: bfloat16 [1024], replicated, may hold values from -1.75 to 1.75
Outputs:
- output: float32 [32, 448, 1024], P('dp')
- grad_tokens: float32 [32, 448, 1024], P('dp')
- grad_encoded: float32 [32, 1500, 1024], P('dp', None, 'tensor')
- grad_self_gain: float32 [1024], replicated
- grad_self_shift: float32 [1024], replicated
- grad_self_query: float32 [1024, 1024], P(None, 'tensor')
- grad_self_query_bias: float32 [1024], P('tensor')
- grad_self_key: float32 [1024, 1024], P(None, 'tensor')
- grad_self_value: float32 [1024, 1024], P(None, 'tensor')
- grad_self_value_bias: float32 [1024], P('tensor')
- grad_self_mixer: float32 [1024, 1024], P('tensor')
- grad_self_mixer_bias: float32 [1024], replicated
- grad_cross_gain: float32 [1024], replicated
- grad_cross_shift: float32 [1024], replicated
- grad_cross_query: float32 [1024, 1024], P(None, 'tensor')
- grad_cross_query_bias: float32 [1024], P('tensor')
- grad_cross_key: float32 [1024, 1024], P(None, 'tensor')
- grad_cross_value: float32 [1024, 1024], P(None, 'tensor')
- grad_cross_value_bias: float32 [1024], P('tensor')
- grad_cross_mixer: float32 [1024, 1024], P('tensor')
- grad_cross_mixer_bias: float32 [1024], replicated
- grad_feed_gain: float32 [1024], replicated
- grad_feed_shift: float32 [1024], replicated
- grad_expand_weight: float32 [1024, 4096], P(None, 'tensor')
- grad_expand_bias: float32 [4096], P('tensor')
- grad_reduce_weight: float32 [4096, 1024], P('tensor')
- grad_reduce_bias: float32 [1024], replicated
All inputs are finite; a program needn't handle non-finite values.
Results may differ from a plain program's by a relative error of at most 0.022.
Values may be sent and summed in bfloat16 or wider, within the bound.
No kernel may reach another device: no remote copies, remote signals or barrier semaphores. Data moves between devices by JAX's collectives and lax.ppermute only.
A program may use at most 256 MiB of HBM per device.

v0:
```python
import math
import jax
import jax.numpy as jnp
from jax import lax
from jax.sharding import PartitionSpec as P

HEAD = 64
EPSILON = 1e-05
F32 = jnp.float32
BF16 = jnp.bfloat16


def normalize(values, norm_gain, norm_shift):
    row_mean = jnp.mean(values, axis=-1, keepdims=True)
    centered = values - row_mean
    spread = jnp.mean(centered * centered, axis=-1, keepdims=True)
    inverse = lax.rsqrt(spread + EPSILON)
    normed = centered * inverse
    return (normed * norm_gain + norm_shift, normed, inverse)


def normalize_back(grad_out, normed, inverse, norm_gain):
    scaled = grad_out * norm_gain
    centre = jnp.mean(scaled, axis=-1, keepdims=True)
    row_along = jnp.mean(scaled * normed, axis=-1, keepdims=True)
    grad_in = inverse * (scaled - centre - normed * row_along)
    return (grad_in, jnp.sum(grad_out * normed, axis=0), jnp.sum(grad_out, axis=0))


def scores_of(queries, key_heads, causal):
    scaling = 1.0 / math.sqrt(queries.shape[-1])
    scores = jnp.einsum("lhe,khe->hlk", queries, key_heads, preferred_element_type=F32) * scaling
    if causal:
        row_index = lax.broadcasted_iota(jnp.int32, scores.shape[-2:], 0)
        col_index = lax.broadcasted_iota(jnp.int32, scores.shape[-2:], 1)
        scores = jnp.where(col_index <= row_index, scores, -1e30)
    return scores


def attend(queries, key_heads, value_heads, causal):
    scores = scores_of(queries, key_heads, causal)
    highest = jnp.max(scores, axis=-1, keepdims=True)
    denominator = jnp.sum(jnp.exp(scores - highest), axis=-1, keepdims=True)
    logsum = highest + jnp.log(denominator)
    probs = jnp.exp(scores - logsum)
    mixture = jnp.einsum(
        "hlk,khe->lhe", probs.astype(BF16), value_heads, preferred_element_type=F32
    )
    return (mixture.astype(BF16), logsum)


def attend_back(grad_mixture, queries, key_heads, value_heads, logsum, causal):
    scaling = 1.0 / math.sqrt(queries.shape[-1])
    probs = jnp.exp(scores_of(queries, key_heads, causal) - logsum)
    grad_probs = jnp.einsum("lhe,khe->hlk", grad_mixture, value_heads, preferred_element_type=F32)
    row_dot = jnp.sum(grad_probs * probs, axis=-1, keepdims=True)
    grad_scores = (probs * (grad_probs - row_dot)).astype(BF16)
    grad_queries = (
        jnp.einsum("hlk,khe->lhe", grad_scores, key_heads, preferred_element_type=F32) * scaling
    ).astype(BF16)
    grad_keys = (
        jnp.einsum("hlk,lhe->khe", grad_scores, queries, preferred_element_type=F32) * scaling
    ).astype(BF16)
    grad_values = jnp.einsum(
        "hlk,lhe->khe", probs.astype(BF16), grad_mixture, preferred_element_type=F32
    ).astype(BF16)
    return (grad_queries, grad_keys, grad_values)


def project(inputs, weight):
    return jnp.dot(inputs, weight, preferred_element_type=F32)


def project_back(grads, weight):
    return jnp.einsum("lc,dc->ld", grads, weight, preferred_element_type=F32)


def weight_grad(inputs, grads):
    left = jnp.concatenate(inputs, axis=0)
    right = jnp.concatenate(grads, axis=0)
    return jnp.einsum("ld,lc->dc", left, right, preferred_element_type=F32).astype(BF16)


def column_sum(grads):
    return jnp.sum(grads.astype(F32), axis=0)


def tensor_sum(partial):
    if lax.axis_size("tensor") != 2:
        return lax.psum(partial, "tensor")
    mine = lax.optimization_barrier(partial.astype(BF16))
    other = lax.ppermute(mine, "tensor", [(0, 1), (1, 0)])
    return mine.astype(F32) + other.astype(F32)


def dp_sum(grads):
    share = lax.psum_scatter(grads, "dp", scatter_dimension=0, tiled=True)
    return lax.all_gather(share, "dp", axis=0, tiled=True)


def local(
    tokens,
    encoded,
    cotangent,
    self_gain,
    self_shift,
    self_query,
    self_query_bias,
    self_key,
    self_value,
    self_value_bias,
    self_mixer,
    self_mixer_bias,
    cross_gain,
    cross_shift,
    cross_query,
    cross_query_bias,
    cross_key,
    cross_value,
    cross_value_bias,
    cross_mixer,
    cross_mixer_bias,
    feed_gain,
    feed_shift,
    expand_weight,
    expand_bias,
    reduce_weight,
    reduce_bias,
):
    clips, length, width = tokens.shape
    frames = encoded.shape[1]
    local_width = self_query.shape[1]
    head_count = local_width // HEAD
    gain_one = self_gain.astype(F32)
    gain_two = cross_gain.astype(F32)
    gain_three = feed_gain.astype(F32)
    each = range(clips)

    def heads(values):
        return values.reshape(values.shape[0], head_count, HEAD)

    def flat(values):
        return values.reshape(values.shape[0], local_width)

    source, normed_one, inverse_one, attn_in = ([], [], [], [])
    self_queries, self_keys, self_values = ([], [], [])
    self_mixture, self_logsum, self_sum = ([], [], [])
    cross_keys, cross_values = ([], [])
    for i in each:
        source.append(tokens[i].astype(F32))
        normed, plain, inverse = normalize(source[i], gain_one, self_shift.astype(F32))
        normed_one.append(plain)
        inverse_one.append(inverse)
        attn_in.append(normed.astype(BF16))
        self_queries.append(
            (project(attn_in[i], self_query) + self_query_bias.astype(F32)).astype(BF16)
        )
        self_keys.append(project(attn_in[i], self_key).astype(BF16))
        self_values.append(
            (project(attn_in[i], self_value) + self_value_bias.astype(F32)).astype(BF16)
        )
        mixed, logsum = attend(
            heads(self_queries[i]), heads(self_keys[i]), heads(self_values[i]), True
        )
        self_mixture.append(flat(mixed))
        self_logsum.append(logsum)
        self_sum.append(tensor_sum(project(self_mixture[i], self_mixer)))
    for i in each:
        cross_keys.append(project(encoded[i], cross_key).astype(BF16))
        cross_values.append(
            (project(encoded[i], cross_value) + cross_value_bias.astype(F32)).astype(BF16)
        )
    hidden_one, normed_two, inverse_two, cross_in = ([], [], [], [])
    cross_queries, cross_mixture, cross_logsum, cross_sum = ([], [], [], [])
    for i in each:
        hidden_one.append(source[i] + self_sum[i] + self_mixer_bias.astype(F32))
        normed, plain, inverse = normalize(hidden_one[i], gain_two, cross_shift.astype(F32))
        normed_two.append(plain)
        inverse_two.append(inverse)
        cross_in.append(normed.astype(BF16))
        cross_queries.append(
            (project(cross_in[i], cross_query) + cross_query_bias.astype(F32)).astype(BF16)
        )
        mixed, logsum = attend(
            heads(cross_queries[i]), heads(cross_keys[i]), heads(cross_values[i]), False
        )
        cross_mixture.append(flat(mixed))
        cross_logsum.append(logsum)
        cross_sum.append(tensor_sum(project(cross_mixture[i], cross_mixer)))
    hidden_two, normed_three, inverse_three, feed_in = ([], [], [], [])
    activated, grad_preact, feed_grad, feed_sum = ([], [], [], [])
    for i in each:
        hidden_two.append(hidden_one[i] + cross_sum[i] + cross_mixer_bias.astype(F32))
        normed, plain, inverse = normalize(hidden_two[i], gain_three, feed_shift.astype(F32))
        normed_three.append(plain)
        inverse_three.append(inverse)
        feed_in.append(normed.astype(BF16))
        preact = project(feed_in[i], expand_weight) + expand_bias.astype(F32)
        grad_activated = project_back(cotangent[i], reduce_weight)
        cdf = 0.5 * (1.0 + lax.erf(preact * (1.0 / math.sqrt(2.0))))
        density = jnp.exp(-0.5 * preact * preact) * (1.0 / math.sqrt(2.0 * math.pi))
        activated.append((preact * cdf).astype(BF16))
        grad_preact.append((grad_activated * (cdf + preact * density)).astype(BF16))
        feed_grad.append(tensor_sum(project_back(grad_preact[i], expand_weight)))
    for i in each:
        feed_sum.append(tensor_sum(project(activated[i], reduce_weight)))
    output = [hidden_two[i] + feed_sum[i] + reduce_bias.astype(F32) for i in each]
    grad_out = [cotangent[i].astype(F32) for i in each]
    grad_reduce_weight = dp_sum(weight_grad(activated, [cotangent[i] for i in each]))
    grad_expand_weight = dp_sum(weight_grad(feed_in, grad_preact))
    grad_reduce_bias = sum((jnp.sum(grad_out[i], axis=0) for i in each))
    grad_expand_bias = sum((column_sum(grad_preact[i]) for i in each))
    grad_two, two_rounded, feed_gains, feed_shifts = ([], [], [], [])
    cross_query_grad, cross_key_grad, cross_value_grad = ([], [], [])
    cross_grad = []
    for i in each:
        norm_grad, part_gain, part_shift = normalize_back(
            feed_grad[i], normed_three[i], inverse_three[i], gain_three
        )
        feed_gains.append(part_gain)
        feed_shifts.append(part_shift)
        grad_two.append(grad_out[i] + norm_grad)
        two_rounded.append(grad_two[i].astype(BF16))
        grad_cross_mixture = project_back(two_rounded[i], cross_mixer).astype(BF16)
        query_grad, key_grad, value_grad = attend_back(
            heads(grad_cross_mixture),
            heads(cross_queries[i]),
            heads(cross_keys[i]),
            heads(cross_values[i]),
            cross_logsum[i],
            False,
        )
        cross_query_grad.append(flat(query_grad))
        cross_key_grad.append(flat(key_grad))
        cross_value_grad.append(flat(value_grad))
        cross_grad.append(tensor_sum(project_back(cross_query_grad[i], cross_query)))
    grad_cross_mixer = dp_sum(weight_grad(cross_mixture, two_rounded))
    grad_cross_query = dp_sum(weight_grad(cross_in, cross_query_grad))
    frames_in = [encoded[i] for i in each]
    grad_cross_key = dp_sum(weight_grad(frames_in, cross_key_grad))
    grad_cross_value = dp_sum(weight_grad(frames_in, cross_value_grad))
    part_cross_mixer_bias = sum((jnp.sum(grad_two[i], axis=0) for i in each))
    grad_cross_query_bias = sum((column_sum(cross_query_grad[i]) for i in each))
    grad_cross_value_bias = sum((column_sum(cross_value_grad[i]) for i in each))
    grad_one, one_rounded, cross_gains, cross_shifts = ([], [], [], [])
    query_grads, key_grads, value_grads, self_grad = ([], [], [], [])
    for i in each:
        norm_grad, part_gain, part_shift = normalize_back(
            cross_grad[i], normed_two[i], inverse_two[i], gain_two
        )
        cross_gains.append(part_gain)
        cross_shifts.append(part_shift)
        grad_one.append(grad_two[i] + norm_grad)
        one_rounded.append(grad_one[i].astype(BF16))
        grad_self_mixture = project_back(one_rounded[i], self_mixer).astype(BF16)
        query_grad, key_grad, value_grad = attend_back(
            heads(grad_self_mixture),
            heads(self_queries[i]),
            heads(self_keys[i]),
            heads(self_values[i]),
            self_logsum[i],
            True,
        )
        query_grads.append(flat(query_grad))
        key_grads.append(flat(key_grad))
        value_grads.append(flat(value_grad))
        self_terms = (
            project_back(query_grads[i], self_query)
            + project_back(key_grads[i], self_key)
            + project_back(value_grads[i], self_value)
        )
        self_grad.append(tensor_sum(self_terms))
    grad_self_mixer = dp_sum(weight_grad(self_mixture, one_rounded))
    grad_self_query = dp_sum(weight_grad(attn_in, query_grads))
    grad_self_key = dp_sum(weight_grad(attn_in, key_grads))
    grad_self_value = dp_sum(weight_grad(attn_in, value_grads))
    part_self_mixer_bias = sum((jnp.sum(grad_one[i], axis=0) for i in each))
    grad_self_query_bias = sum((column_sum(query_grads[i]) for i in each))
    grad_self_value_bias = sum((column_sum(value_grads[i]) for i in each))
    grad_encoded = []
    members = lax.axis_size("tensor")
    share = width // members
    for i in each:
        if members == 2:
            me = lax.axis_index("tensor")

            def terms(part):
                rows_key = lax.dynamic_slice_in_dim(cross_key, part * share, share, 0)
                rows_value = lax.dynamic_slice_in_dim(cross_value, part * share, share, 0)
                return project_back(cross_key_grad[i], rows_key) + project_back(
                    cross_value_grad[i], rows_value
                )

            other = lax.ppermute(terms(1 - me).astype(BF16), "tensor", [(0, 1), (1, 0)])
            grad_encoded.append(terms(me) + other.astype(F32))
        else:
            frame_terms = project_back(cross_key_grad[i], cross_key) + project_back(
                cross_value_grad[i], cross_value
            )
            grad_encoded.append(
                lax.psum_scatter(frame_terms, "tensor", scatter_dimension=1, tiled=True)
            )
    self_gains, self_shifts, grad_tokens = ([], [], [])
    for i in each:
        norm_grad, part_gain, part_shift = normalize_back(
            self_grad[i], normed_one[i], inverse_one[i], gain_one
        )
        self_gains.append(part_gain)
        self_shifts.append(part_shift)
        grad_tokens.append(grad_one[i] + norm_grad)
    vectors = [
        sum(self_gains),
        sum(self_shifts),
        part_self_mixer_bias,
        sum(cross_gains),
        sum(cross_shifts),
        part_cross_mixer_bias,
        sum(feed_gains),
        sum(feed_shifts),
        grad_reduce_bias,
        grad_self_query_bias,
        grad_self_value_bias,
        grad_cross_query_bias,
        grad_cross_value_bias,
        grad_expand_bias,
    ]
    summed = lax.psum(jnp.concatenate(vectors), "dp")
    pieces, offset = ([], 0)
    for piece in vectors:
        pieces.append(summed[offset : offset + piece.size])
        offset = offset + piece.size
    return (
        jnp.stack(output),
        jnp.stack(grad_tokens),
        jnp.stack(grad_encoded),
        pieces[0],
        pieces[1],
        grad_self_query.astype(F32),
        pieces[9],
        grad_self_key.astype(F32),
        grad_self_value.astype(F32),
        pieces[10],
        grad_self_mixer.astype(F32),
        pieces[2],
        pieces[3],
        pieces[4],
        grad_cross_query.astype(F32),
        pieces[11],
        grad_cross_key.astype(F32),
        grad_cross_value.astype(F32),
        pieces[12],
        grad_cross_mixer.astype(F32),
        pieces[5],
        pieces[6],
        pieces[7],
        grad_expand_weight.astype(F32),
        pieces[13],
        grad_reduce_weight.astype(F32),
        pieces[8],
    )


def solution(mesh):
    rows = P("dp", None, None)
    column, row, part = (P(None, "tensor"), P("tensor", None), P("tensor"))
    return jax.shard_map(
        local,
        mesh=mesh,
        in_specs=(
            rows,
            rows,
            rows,
            P(),
            P(),
            column,
            part,
            column,
            column,
            part,
            row,
            P(),
            P(),
            P(),
            column,
            part,
            column,
            column,
            part,
            row,
            P(),
            P(),
            P(),
            column,
            part,
            row,
            P(),
        ),
        out_specs=(
            rows,
            rows,
            P("dp", None, "tensor"),
            P(),
            P(),
            column,
            part,
            column,
            column,
            part,
            row,
            P(),
            P(),
            P(),
            column,
            part,
            column,
            column,
            part,
            row,
            P(),
            P(),
            P(),
            column,
            part,
            row,
            P(),
        ),
        check_vma=False,
    )
```

profile of v0, /device:TPU:0, one launch (start us, length us, event | category | flops | bytes accessed | tf_op | source)
XLA Modules:
  0.0 1475.0 jit_solution(17825031323830864179)
XLA Ops:
  41.3 9.7 fusion.219
  51.0 8.1 copy_bitcast_fusion
  86.2 5.9 exponential_reduce_fusion.1
  93.5 12.3 fusion.135
  108.2 21.7 %collective-permute-done.1 = bf16[448,1024]{1,0:T(8,128)(2,1)S(1)} collective-permute-done((bf16[448,1024]{1,0:T(8,128)(2,1)S(1)}, bf16[448,1024]{1,0:T(8,128)(2,1)S(1)}, u32[]{:S(2)}, u32[]{:S(2)}) %collective-permute-start.1) | collective-permute-done | bytes 917536 | tf_op jit(solution)/shard_map/ppermute | solution.py:92
  151.8 15.1 %collective-permute-done.6 = bf16[448,1024]{1,0:T(8,128)(2,1)} collective-permute-done((bf16[448,1024]{1,0:T(8,128)(2,1)}, bf16[448,1024]{1,0:T(8,128)(2,1)}, u32[]{:S(2)}, u32[]{:S(2)}) %collective-permute-start.6) | collective-permute-done | bytes 917536 | tf_op jit(solution)/shard_map/ppermute | solution.py:92
  170.5 13.8 collective-permute-done.2
  194.5 15.2 %multiply_reduce_fusion.1 = (f32[8,448]{1,0:T(8,128)S(1)}, f32[8,448,1500]{2,1,0:T(8,128)}) fusion(f32[8,448,1500]{2,1,0:T(8,128)} %copy-done.1, f32[8,448]{1,0:T(8,128)S(1)} %log_add_fusion.2, bf16[448,8,64]{0,2,1:T(8,128)(2,1)} %bitcast.336, bf16[1500,8,64]{0,2,1:T(8,128)(2,1)} %bitcast.325), kind=kOutput, calls=%fused_computation.3 | convolution fusion | flops 709628416 | bytes 45031424 | tf_op jit(solution)/shard_map/lhe,khe->hlk/dot_general | solution.py:55
  209.7 15.0 %multiply_convert_fusion.1 = bf16[8,448,1500]{2,1,0:T(8,128)(2,1)S(1)} fusion(f32[8,448,1500]{2,1,0:T(8,128)} %get-tuple-element.165, f32[8,448,1500]{2,1,0:T(8,128)} %copy-done.1, f32[8,448]{1,0:T(8,128)S(1)} %get-tuple-element.164, f32[8,448]{1,0:T(8,128)S(1)} %log_add_fusion.2), kind=kLoop, calls=%fused_computation.2 | loop fusion | flops 26880000 | bytes 53788672 | tf_op jit(solution)/shard_map/convert_element_type | solution.py:57
  241.8 5.5 fusion.222
  247.4 5.9 collective-permute-done.7
  264.9 9.1 multiply_reduce_fusion.5
  316.1 5.7 exponential_reduce_fusion
  324.0 10.1 fusion.138
  337.3 10.9 convert_reduce_fusion.3
  348.3 6.3 collective-permute-done.4
  374.0 15.8 %collective-permute-done.9 = bf16[448,1024]{1,0:T(8,128)(2,1)S(1)} collective-permute-done((bf16[448,1024]{1,0:T(8,128)(2,1)S(1)}, bf16[448,1024]{1,0:T(8,128)(2,1)S(1)}, u32[]{:S(2)}, u32[]{:S(2)}) %collective-permute-start.9) | collective-permute-done | bytes 917536 | tf_op jit(solution)/shard_map/ppermute | solution.py:92
  391.3 12.4 collective-permute-done.5
  416.4 11.9 convert_reduce_fusion.2
  429.6 5.4 fusion.113
  435.0 15.4 %multiply_reduce_fusion = (f32[8,448]{1,0:T(8,128)S(1)}, f32[8,448,1500]{2,1,0:T(8,128)}) fusion(f32[8,448,1500]{2,1,0:T(8,128)} %copy-done.2, f32[8,448]{1,0:T(8,128)S(1)} %log_add_fusion, bf16[448,8,64]{0,2,1:T(8,128)(2,1)} %bitcast.339, bf16[1500,8,64]{0,2,1:T(8,128)(2,1)} %bitcast.322), kind=kOutput, calls=%fused_computation.1 | convolution fusion | flops 709628416 | bytes 45031424 | tf_op jit(solution)/shard_map/lhe,khe->hlk/dot_general | solution.py:55
  450.9 14.9 %multiply_convert_fusion = bf16[8,448,1500]{2,1,0:T(8,128)(2,1)S(1)} fusion(f32[8,448,1500]{2,1,0:T(8,128)} %get-tuple-element.172, f32[8,448,1500]{2,1,0:T(8,128)} %copy-done.2, f32[8,448]{1,0:T(8,128)S(1)} %get-tuple-element.171, f32[8,448]{1,0:T(8,128)S(1)} %log_add_fusion), kind=kLoop, calls=%fused_computation | loop fusion | flops 26880000 | bytes 53788672 | tf_op jit(solution)/shard_map/convert_element_type | solution.py:57
  479.2 8.1 convert_reduce_fusion.8
  490.6 5.9 convert_reduce_fusion.11
  499.3 6.6 collective-permute-done.10
  552.2 6.2 convolution_convert_fusion
  559.8 8.2 convolution_convert_fusion.1
  569.4 23.4 %reduce-scatter.21.cloned.1.call-done = bf16[64,512]{1,0:T(8,128)(2,1)} async-done(((bf16[1024,512]{1,0:T(8,128)(2,1)}), bf16[64,512]{1,0:T(8,128)(2,1)}) %reduce-scatter.21.cloned.1.call-update) | async-done | bytes 65552 | tf_op jit(solution)/shard_map/reduce_scatter | solution.py:97
  592.8 60.1 %reduce-scatter.19.cloned.1.call-done = bf16[64,512]{1,0:T(8,128)(2,1)} async-done(((bf16[1024,512]{1,0:T(8,128)(2,1)}), bf16[64,512]{1,0:T(8,128)(2,1)}) %reduce-scatter.19.cloned.1.call-update) | async-done | bytes 65552 | tf_op jit(solution)/shard_map/reduce_scatter | solution.py:97
  652.9 60.1 %reduce-scatter.15.cloned.1.call-done = bf16[64,512]{1,0:T(8,128)(2,1)} async-done(((bf16[1024,512]{1,0:T(8,128)(2,1)}), bf16[64,512]{1,0:T(8,128)(2,1)}) %reduce-scatter.15.cloned.1.call-update) | async-done | bytes 65552 | tf_op jit(solution)/shard_map/reduce_scatter | solution.py:97
  713.1 60.1 %reduce-scatter.17.cloned.1.call-done = bf16[32,1024]{1,0:T(8,128)(2,1)} async-done(((bf16[512,1024]{1,0:T(8,128)(2,1)}), bf16[32,1024]{1,0:T(8,128)(2,1)}) %reduce-scatter.17.cloned.1.call-update) | async-done | bytes 65552 | tf_op jit(solution)/shard_map/reduce_scatter | solution.py:97
  773.2 60.8 %reduce-scatter.11.cloned.1.call-done = bf16[64,512]{1,0:T(8,128)(2,1)} async-done(((bf16[1024,512]{1,0:T(8,128)(2,1)}), bf16[64,512]{1,0:T(8,128)(2,1)}) %reduce-scatter.11.cloned.1.call-update) | async-done | bytes 65552 | tf_op jit(solution)/shard_map/reduce_scatter | solution.py:97
  834.1 60.7 %reduce-scatter.13.cloned.1.call-done = bf16[64,512]{1,0:T(8,128)(2,1)} async-done(((bf16[1024,512]{1,0:T(8,128)(2,1)}), bf16[64,512]{1,0:T(8,128)(2,1)}) %reduce-scatter.13.cloned.1.call-update) | async-done | bytes 65552 | tf_op jit(solution)/shard_map/reduce_scatter | solution.py:97
  894.9 76.2 %reduce-scatter.29.cloned.1.call-done = bf16[128,1024]{1,0:T(8,128)(2,1)} async-done(((bf16[2048,1024]{1,0:T(8,128)(2,1)}), bf16[128,1024]{1,0:T(8,128)(2,1)}) %reduce-scatter.29.cloned.1.call-update) | async-done | bytes 262160 | tf_op jit(solution)/shard_map/reduce_scatter | solution.py:97
  983.4 29.0 %collective-permute-done.12 = bf16[1500,512]{1,0:T(8,128)(2,1)} collective-permute-done((bf16[1500,512]{1,0:T(8,128)(2,1)}, bf16[1500,512]{1,0:T(8,128)(2,1)}, u32[]{:S(2)}, u32[]{:S(2)}) %collective-permute-start.12) | collective-permute-done | bytes 1536032 | tf_op jit(solution)/shard_map/ppermute | solution.py:294
  1019.2 28.0 %reduce-scatter.27.cloned.1.call-done = bf16[64,2048]{1,0:T(8,128)(2,1)} async-done(((bf16[1024,2048]{1,0:T(8,128)(2,1)}), bf16[64,2048]{1,0:T(8,128)(2,1)}) %reduce-scatter.27.cloned.1.call-update) | async-done | bytes 262160 | tf_op jit(solution)/shard_map/reduce_scatter | solution.py:97
  1063.9 25.0 %collective-permute-done.13 = bf16[1500,512]{1,0:T(8,128)(2,1)} collective-permute-done((bf16[1500,512]{1,0:T(8,128)(2,1)}, bf16[1500,512]{1,0:T(8,128)(2,1)}, u32[]{:S(2)}, u32[]{:S(2)}) %collective-permute-start.13) | collective-permute-done | bytes 1536032 | tf_op jit(solution)/shard_map/ppermute | solution.py:294
  1093.7 12.7 copy.122
  1110.9 57.9 %psum.7 = f32[13312]{0:T(1024)S(1)} all-reduce(f32[13312]{0:T(1024)S(1)} %add_dynamic-update-slice_fusion), channel_id=1, replica_groups=mesh['dp'=16,'tensor'=2] {'dp'}, use_global_device_ids=true, to_apply=%region_64.65 | all-reduce | flops 13312 | bytes 106496 | tf_op jit(solution)/shard_map/psum | solution.py:327
  1185.3 17.9 %all-gather.19.cloned.1.call-done = bf16[1024,512]{1,0:T(8,128)(2,1)} async-done(((bf16[64,512]{1,0:T(8,128)(2,1)}), bf16[1024,512]{1,0:T(8,128)(2,1)}) %all-gather.19.cloned.1.call-update) | async-done | bytes 1048592 | tf_op jit(solution)/shard_map/all_gather | solution.py:98
  1206.1 36.0 %all-gather.15.cloned.1.call-done = bf16[1024,512]{1,0:T(8,128)(2,1)} async-done(((bf16[64,512]{1,0:T(8,128)(2,1)}), bf16[1024,512]{1,0:T(8,128)(2,1)}) %all-gather.15.cloned.1.call-update) | async-done | bytes 1048592 | tf_op jit(solution)/shard_map/all_gather | solution.py:98
  1245.0 36.0 %all-gather.17.cloned.1.call-done = bf16[512,1024]{1,0:T(8,128)(2,1)} async-done(((bf16[32,1024]{1,0:T(8,128)(2,1)}), bf16[512,1024]{1,0:T(8,128)(2,1)}) %all-gather.17.cloned.1.call-update) | async-done | bytes 1048592 | tf_op jit(solution)/shard_map/all_gather | solution.py:98
  1283.8 36.1 %all-gather.11.cloned.1.call-done = bf16[1024,512]{1,0:T(8,128)(2,1)} async-done(((bf16[64,512]{1,0:T(8,128)(2,1)}), bf16[1024,512]{1,0:T(8,128)(2,1)}) %all-gather.11.cloned.1.call-update) | async-done | bytes 1048592 | tf_op jit(solution)/shard_map/all_gather | solution.py:98
  1322.8 36.0 %all-gather.13.cloned.1.call-done = bf16[1024,512]{1,0:T(8,128)(2,1)} async-done(((bf16[64,512]{1,0:T(8,128)(2,1)}), bf16[1024,512]{1,0:T(8,128)(2,1)}) %all-gather.13.cloned.1.call-update) | async-done | bytes 1048592 | tf_op jit(solution)/shard_map/all_gather | solution.py:98
  1361.6 48.7 %all-gather.29.cloned.1.call-done = bf16[2048,1024]{1,0:T(8,128)(2,1)} async-done(((bf16[128,1024]{1,0:T(8,128)(2,1)}), bf16[2048,1024]{1,0:T(8,128)(2,1)}) %all-gather.29.cloned.1.call-update) | async-done | bytes 4194320 | tf_op jit(solution)/shard_map/all_gather | solution.py:98
  1410.3 6.6 convert_element_type.662
  1417.0 44.3 %all-gather.27.cloned.1.call-done = bf16[1024,2048]{1,0:T(8,128)(2,1)} async-done(((bf16[64,2048]{1,0:T(8,128)(2,1)}), bf16[1024,2048]{1,0:T(8,128)(2,1)}) %all-gather.27.cloned.1.call-update) | async-done | bytes 4194320 | tf_op jit(solution)/shard_map/all_gather | solution.py:98
  1461.3 6.7 convert_element_type.660
  (607 shorter events, 354.7 us)
Async XLA Ops:
  7.2 59.2 %copy-start = (bf16[1024,512]{1,0:T(8,128)(2,1)S(1)}, bf16[1024,512]{1,0:T(8,128)(2,1)}, u32[]{:S(2)}) copy-start(bf16[1024,512]{1,0:T(8,128)(2,1)} %param.43) | copy-start | bytes 3145732
  7.2 560.9 %reduce-scatter.25.cloned.1.call-start = ((), (), s32[]{:S(2)}) async-start(), calls=%async_computation.24 | async-start | bytes 1114112 | tf_op jit(solution)/shard_map/reduce_scatter | solution.py:97
  36.5 14.5 copy-start.155
  38.2 35.6 %collective-permute-start = (bf16[448,1024]{1,0:T(8,128)(2,1)}, bf16[448,1024]{1,0:T(8,128)(2,1)}, u32[]{:S(2)}, u32[]{:S(2)}) collective-permute-start(bf16[448,1024]{1,0:T(8,128)(2,1)} %convolution_convert_fusion.14), channel_id=1, source_target_pairs={{0,1},{1,0},{2,3},{3,2},{4,5},{5,4},{6,7},{7,6},{8,9},{9,8},{10,11... | collective-permute-start | bytes 2752520 | tf_op jit(solution)/shard_map/ppermute | solution.py:92
  105.9 24.1 %copy-start.11 = (f32[448,1024]{1,0:T(8,128)S(1)}, f32[448,1024]{1,0:T(8,128)}, u32[]{:S(2)}) copy-start(f32[448,1024]{1,0:T(8,128)} %copy-done.10) | copy-start | bytes 5505028
  108.1 21.9 %collective-permute-start.1 = (bf16[448,1024]{1,0:T(8,128)(2,1)S(1)}, bf16[448,1024]{1,0:T(8,128)(2,1)S(1)}, u32[]{:S(2)}, u32[]{:S(2)}) collective-permute-start(bf16[448,1024]{1,0:T(8,128)(2,1)S(1)} %convolution_convert_fusion.13), channel_id=1, source_target_pairs={{0,1},{1,0},{2,3},{3,2},{4,5},{5,4},{6,7},{7,6},{8,9},{9,8},{10,11... | collective-permute-start | bytes 2752520 | tf_op jit(solution)/shard_map/ppermute | solution.py:92
  143.3 23.5 %collective-permute-start.6 = (bf16[448,1024]{1,0:T(8,128)(2,1)}, bf16[448,1024]{1,0:T(8,128)(2,1)}, u32[]{:S(2)}, u32[]{:S(2)}) collective-permute-start(bf16[448,1024]{1,0:T(8,128)(2,1)} %convolution_convert_fusion.16), channel_id=1, source_target_pairs={{0,1},{1,0},{2,3},{3,2},{4,5},{5,4},{6,7},{7,6},{8,9},{9,8},{10,11... | collective-permute-start | bytes 2752520 | tf_op jit(solution)/shard_map/ppermute | solution.py:92
  146.6 37.6 %collective-permute-start.2 = (bf16[448,1024]{1,0:T(8,128)(2,1)}, bf16[448,1024]{1,0:T(8,128)(2,1)}, u32[]{:S(2)}, u32[]{:S(2)}) collective-permute-start(bf16[448,1024]{1,0:T(8,128)(2,1)} %convolution_convert_fusion.18), channel_id=1, source_target_pairs={{0,1},{1,0},{2,3},{3,2},{4,5},{5,4},{6,7},{7,6},{8,9},{9,8},{10,11... | collective-permute-start | bytes 2752520 | tf_op jit(solution)/shard_map/ppermute | solution.py:92
  151.8 32.5 %copy-start.14 = (f32[448,1024]{1,0:T(8,128)S(1)}, f32[448,1024]{1,0:T(8,128)}, u32[]{:S(2)}) copy-start(f32[448,1024]{1,0:T(8,128)} %copy-done.13) | copy-start | bytes 5505028
  151.8 32.5 %copy-start.37 = (bf16[2,448,1024]{2,1,0:T(8,128)(2,1)S(1)}, bf16[2,448,1024]{2,1,0:T(8,128)(2,1)}, u32[]{:S(2)}) copy-start(bf16[2,448,1024]{2,1,0:T(8,128)(2,1)} %param.29) | copy-start | bytes 5505028
  209.7 15.0 %copy-start.22 = (bf16[1500,512]{0,1:T(8,128)(2,1)S(1)}, bf16[1500,512]{0,1:T(8,128)(2,1)}, u32[]{:S(2)}) copy-start(bf16[1500,512]{0,1:T(8,128)(2,1)} %copy.103) | copy-start | bytes 4608004
  232.9 20.4 %collective-permute-start.7 = (bf16[448,1024]{1,0:T(8,128)(2,1)}, bf16[448,1024]{1,0:T(8,128)(2,1)}, u32[]{:S(2)}, u32[]{:S(2)}) collective-permute-start(bf16[448,1024]{1,0:T(8,128)(2,1)} %convolution_convert_fusion.10), channel_id=1, source_target_pairs={{0,1},{1,0},{2,3},{3,2},{4,5},{5,4},{6,7},{7,6},{8,9},{9,8},{10,11... | collective-permute-start | bytes 2752520 | tf_op jit(solution)/shard_map/ppermute | solution.py:92
  284.8 19.5 %collective-permute-start.3 = (bf16[448,1024]{1,0:T(8,128)(2,1)}, bf16[448,1024]{1,0:T(8,128)(2,1)}, u32[]{:S(2)}, u32[]{:S(2)}) collective-permute-start(bf16[448,1024]{1,0:T(8,128)(2,1)} %convolution_convert_fusion.12), channel_id=1, source_target_pairs={{0,1},{1,0},{2,3},{3,2},{4,5},{5,4},{6,7},{7,6},{8,9},{9,8},{10,11... | collective-permute-start | bytes 2752520 | tf_op jit(solution)/shard_map/ppermute | solution.py:92
  336.2 18.5 %copy-start.9 = (f32[448,1024]{1,0:T(8,128)S(1)}, f32[448,1024]{1,0:T(8,128)}, u32[]{:S(2)}) copy-start(f32[448,1024]{1,0:T(8,128)} %copy-done.8) | copy-start | bytes 5505028
  336.2 18.4 %collective-permute-start.4 = (bf16[448,1024]{1,0:T(8,128)(2,1)S(1)}, bf16[448,1024]{1,0:T(8,128)(2,1)S(1)}, u32[]{:S(2)}, u32[]{:S(2)}) collective-permute-start(bf16[448,1024]{1,0:T(8,128)(2,1)S(1)} %convolution_convert_fusion.11), channel_id=1, source_target_pairs={{0,1},{1,0},{2,3},{3,2},{4,5},{5,4},{6,7},{7,6},{8,9},{9,8},{10,11... | collective-permute-start | bytes 2752520 | tf_op jit(solution)/shard_map/ppermute | solution.py:92
  366.5 23.3 %collective-permute-start.9 = (bf16[448,1024]{1,0:T(8,128)(2,1)S(1)}, bf16[448,1024]{1,0:T(8,128)(2,1)S(1)}, u32[]{:S(2)}, u32[]{:S(2)}) collective-permute-start(bf16[448,1024]{1,0:T(8,128)(2,1)S(1)} %convolution_convert_fusion.15), channel_id=1, source_target_pairs={{0,1},{1,0},{2,3},{3,2},{4,5},{5,4},{6,7},{7,6},{8,9},{9,8},{10,11... | collective-permute-start | bytes 2752520 | tf_op jit(solution)/shard_map/ppermute | solution.py:92
  370.0 33.7 %collective-permute-start.5 = (bf16[448,1024]{1,0:T(8,128)(2,1)S(1)}, bf16[448,1024]{1,0:T(8,128)(2,1)S(1)}, u32[]{:S(2)}, u32[]{:S(2)}) collective-permute-start(bf16[448,1024]{1,0:T(8,128)(2,1)S(1)} %convolution_convert_fusion.17), channel_id=1, source_target_pairs={{0,1},{1,0},{2,3},{3,2},{4,5},{5,4},{6,7},{7,6},{8,9},{9,8},{10,11... | collective-permute-start | bytes 2752520 | tf_op jit(solution)/shard_map/ppermute | solution.py:92
  414.1 154.7 %reduce-scatter.23.cloned.1.call-start = ((), (), s32[]{:S(2)}) async-start(), calls=%async_computation.22 | async-start | bytes 1114112 | tf_op jit(solution)/shard_map/reduce_scatter | solution.py:97
  450.4 142.3 %reduce-scatter.21.cloned.1.call-start = ((), (), s32[]{:S(2)}) async-start(), calls=%async_computation.20 | async-start | bytes 1114112 | tf_op jit(solution)/shard_map/reduce_scatter | solution.py:97
  450.9 15.0 %copy-start.41 = (bf16[448,512]{0,1:T(8,128)(2,1)S(1)}, bf16[448,512]{0,1:T(8,128)(2,1)}, u32[]{:S(2)}) copy-start(bf16[448,512]{0,1:T(8,128)(2,1)} %copy.110) | copy-start | bytes 1376260
  479.1 173.8 %reduce-scatter.19.cloned.1.call-start = ((), (), s32[]{:S(2)}) async-start(), calls=%async_computation.18 | async-start | bytes 1114112 | tf_op jit(solution)/shard_map/reduce_scatter | solution.py:97
  489.0 16.9 %collective-permute-start.10 = (bf16[448,1024]{1,0:T(8,128)(2,1)}, bf16[448,1024]{1,0:T(8,128)(2,1)}, u32[]{:S(2)}, u32[]{:S(2)}) collective-permute-start(bf16[448,1024]{1,0:T(8,128)(2,1)} %convolution_convert_fusion.9), channel_id=1, source_target_pairs={{0,1},{1,0},{2,3},{3,2},{4,5},{5,4},{6,7},{7,6},{8,9},{9,8},{10,11... | collective-permute-start | bytes 2752520 | tf_op jit(solution)/shard_map/ppermute | solution.py:92
  499.1 214.0 %reduce-scatter.15.cloned.1.call-start = ((), (), s32[]{:S(2)}) async-start(), calls=%async_computation.14 | async-start | bytes 1114112 | tf_op jit(solution)/shard_map/reduce_scatter | solution.py:97
  522.5 250.7 %reduce-scatter.17.cloned.1.call-start = ((), (), s32[]{:S(2)}) async-start(), calls=%async_computation.16 | async-start | bytes 1114112 | tf_op jit(solution)/shard_map/reduce_scatter | solution.py:97
  525.6 13.2 copy-start.73
  527.9 306.1 %reduce-scatter.11.cloned.1.call-start = ((), (), s32[]{:S(2)}) async-start(), calls=%async_computation.10 | async-start | bytes 1114112 | tf_op jit(solution)/shard_map/reduce_scatter | solution.py:97
  542.2 352.6 %reduce-scatter.13.cloned.1.call-start = ((), (), s32[]{:S(2)}) async-start(), calls=%async_computation.12 | async-start | bytes 1114112 | tf_op jit(solution)/shard_map/reduce_scatter | solution.py:97
  550.0 421.1 %reduce-scatter.29.cloned.1.call-start = ((), (), s32[]{:S(2)}) async-start(), calls=%async_computation.28 | async-start | bytes 4456448 | tf_op jit(solution)/shard_map/reduce_scatter | solution.py:97
  558.4 488.8 %reduce-scatter.27.cloned.1.call-start = ((), (), s32[]{:S(2)}) async-start(), calls=%async_computation.26 | async-start | bytes 4456448 | tf_op jit(solution)/shard_map/reduce_scatter | solution.py:97
  568.0 403.6 %copy-start.18 = (bf16[8,64,1500]{2,1,0:T(8,128)(2,1)S(1)}, bf16[8,64,1500]{2,1,0:T(8,128)(2,1)}, u32[]{:S(2)}) copy-start(bf16[8,64,1500]{2,1,0:T(8,128)(2,1)} %fusion.32) | copy-start | bytes 4608004
  568.0 608.8 %all-gather.25.cloned.1.call-start = ((), (), s32[]{:S(2)}) async-start(), calls=%async_computation.25 | async-start | bytes 1114112 | tf_op jit(solution)/shard_map/all_gather | solution.py:98
  568.8 610.9 %all-gather.23.cloned.1.call-start = ((), (), s32[]{:S(2)}) async-start(), calls=%async_computation.23 | async-start | bytes 1114112 | tf_op jit(solution)/shard_map/all_gather | solution.py:98
  569.3 613.2 %all-gather.21.cloned.1.call-start = ((), (), s32[]{:S(2)}) async-start(), calls=%async_computation.21 | async-start | bytes 1114112 | tf_op jit(solution)/shard_map/all_gather | solution.py:98
  592.8 610.5 %all-gather.19.cloned.1.call-start = ((), (), s32[]{:S(2)}) async-start(), calls=%async_computation.19 | async-start | bytes 1114112 | tf_op jit(solution)/shard_map/all_gather | solution.py:98
  652.9 589.3 %all-gather.15.cloned.1.call-start = ((), (), s32[]{:S(2)}) async-start(), calls=%async_computation.15 | async-start | bytes 1114112 | tf_op jit(solution)/shard_map/all_gather | solution.py:98
  713.0 568.0 %all-gather.17.cloned.1.call-start = ((), (), s32[]{:S(2)}) async-start(), calls=%async_computation.17 | async-start | bytes 1114112 | tf_op jit(solution)/shard_map/all_gather | solution.py:98
  773.2 546.7 %all-gather.11.cloned.1.call-start = ((), (), s32[]{:S(2)}) async-start(), calls=%async_computation.11 | async-start | bytes 1114112 | tf_op jit(solution)/shard_map/all_gather | solution.py:98
  834.0 524.8 %all-gather.13.cloned.1.call-start = ((), (), s32[]{:S(2)}) async-start(), calls=%async_computation.13 | async-start | bytes 1114112 | tf_op jit(solution)/shard_map/all_gather | solution.py:98
  894.8 515.5 %all-gather.29.cloned.1.call-start = ((), (), s32[]{:S(2)}) async-start(), calls=%async_computation.29 | async-start | bytes 4456448 | tf_op jit(solution)/shard_map/all_gather | solution.py:98
  971.1 490.2 %all-gather.27.cloned.1.call-start = ((), (), s32[]{:S(2)}) async-start(), calls=%async_computation.27 | async-start | bytes 4456448 | tf_op jit(solution)/shard_map/all_gather | solution.py:98
  975.5 36.9 %collective-permute-start.12 = (bf16[1500,512]{1,0:T(8,128)(2,1)}, bf16[1500,512]{1,0:T(8,128)(2,1)}, u32[]{:S(2)}, u32[]{:S(2)}) collective-permute-start(bf16[1500,512]{1,0:T(8,128)(2,1)} %fusion.36), channel_id=1, source_target_pairs={{0,1},{1,0},{2,3},{3,2},{4,5},{5,4},{6,7},{7,6},{8,9},{9,8},{10,11... | collective-permute-start | bytes 4608008 | tf_op jit(solution)/shard_map/ppermute | solution.py:294
  981.1 31.3 %copy-start.32 = (bf16[8,64,1500]{2,1,0:T(8,128)(2,1)S(1)}, bf16[8,64,1500]{2,1,0:T(8,128)(2,1)}, u32[]{:S(2)}) copy-start(bf16[8,64,1500]{2,1,0:T(8,128)(2,1)} %get-tuple-element.188) | copy-start | bytes 4608004
  981.1 31.3 %copy-start.60 = (bf16[1024,512]{1,0:T(8,128)(2,1)S(1)}, bf16[1024,512]{1,0:T(8,128)(2,1)}, u32[]{:S(2)}) copy-start(bf16[1024,512]{1,0:T(8,128)(2,1)} %param.44) | copy-start | bytes 3145732
  982.8 33.7 %copy-start.20 = (bf16[8,64,1500]{2,1,0:T(8,128)(2,1)S(1)}, bf16[8,64,1500]{2,1,0:T(8,128)(2,1)}, u32[]{:S(2)}) copy-start(bf16[8,64,1500]{2,1,0:T(8,128)(2,1)} %copy-done.19) | copy-start | bytes 4608004
  982.8 123.6 %collective-permute-start.8 = (bf16[448,1024]{1,0:T(8,128)(2,1)}, bf16[448,1024]{1,0:T(8,128)(2,1)}, u32[]{:S(2)}, u32[]{:S(2)}) collective-permute-start(bf16[448,1024]{1,0:T(8,128)(2,1)} %add_convert_fusion.1), channel_id=1, source_target_pairs={{0,1},{1,0},{2,3},{3,2},{4,5},{5,4},{6,7},{7,6},{8,9},{9,8},{10,11... | collective-permute-start | bytes 2752520 | tf_op jit(solution)/shard_map/ppermute | solution.py:92
  1052.0 36.9 %collective-permute-start.13 = (bf16[1500,512]{1,0:T(8,128)(2,1)}, bf16[1500,512]{1,0:T(8,128)(2,1)}, u32[]{:S(2)}, u32[]{:S(2)}) collective-permute-start(bf16[1500,512]{1,0:T(8,128)(2,1)} %fusion.37), channel_id=1, source_target_pairs={{0,1},{1,0},{2,3},{3,2},{4,5},{5,4},{6,7},{7,6},{8,9},{9,8},{10,11... | collective-permute-start | bytes 4608008 | tf_op jit(solution)/shard_map/ppermute | solution.py:294
  1060.7 45.8 %collective-permute-start.11 = (bf16[448,1024]{1,0:T(8,128)(2,1)}, bf16[448,1024]{1,0:T(8,128)(2,1)}, u32[]{:S(2)}, u32[]{:S(2)}) collective-permute-start(bf16[448,1024]{1,0:T(8,128)(2,1)} %add_convert_fusion), channel_id=1, source_target_pairs={{0,1},{1,0},{2,3},{3,2},{4,5},{5,4},{6,7},{7,6},{8,9},{9,8},{10,11... | collective-permute-start | bytes 2752520 | tf_op jit(solution)/shard_map/ppermute | solution.py:92
  1061.3 27.6 %copy-start.34 = (bf16[8,64,1500]{2,1,0:T(8,128)(2,1)S(1)}, bf16[8,64,1500]{2,1,0:T(8,128)(2,1)}, u32[]{:S(2)}) copy-start(bf16[8,64,1500]{2,1,0:T(8,128)(2,1)} %copy-done.33) | copy-start | bytes 4608004
  (160 other events, 653.6 us)
Sparse Core Ops, SparseCore 0:
  414.3 57.9 reduce-scatter.24
  475.8 56.7 reduce-scatter.22
  536.3 56.4 reduce-scatter.20
  596.2 56.6 reduce-scatter.18
  656.3 56.6 reduce-scatter.14
  716.5 56.6 reduce-scatter.16
  777.4 56.6 reduce-scatter.10
  838.2 56.5 reduce-scatter.12
  899.2 71.8 reduce-scatter.28
  975.4 71.8 reduce-scatter.26
  1049.4 36.9 all-gather.24
  1088.4 36.8 all-gather.22
  1127.5 36.8 all-gather.20
  1166.4 36.7 all-gather.18
  1205.3 36.8 all-gather.14
  1244.2 36.8 all-gather.16
  1283.1 36.8 all-gather.10
  1321.9 36.8 all-gather.12
  1361.0 49.3 all-gather.28
  1412.4 48.8 all-gather.26
where the time goes:
time: 1480 us; the launch traced here: 1470 us
  waiting for transfers between devices  843 us (57%)
  matrix products  294 us (20%)
  other arithmetic  140 us (9%)
  local copies, waits for them, and re-layouts  105 us (7%)
  blocking collectives  57.9 us (4%)
  starting transfers between devices  17.7 us (1%)
  between operations  16.5 us (1%)
    reduce_scatter x10, waiting for transfers between devices, dp_sum(): share = lax.psum_scatter(grads, 'dp', scatter_dimension=0, tiled=True)  429 us
    all_gather x10, waiting for transfers between devices, dp_sum(): return lax.all_gather(share, 'dp', axis=0, tiled=True)  255 us
    ppermute x12, waiting for transfers between devices, tensor_sum(): other = lax.ppermute(mine, 'tensor', [(0, 1), (1, 0)])  103 us
    psum x1, blocking collectives, local(): summed = lax.psum(jnp.concatenate(vectors), 'dp')  57.9 us
    ppermute x2, waiting for transfers between devices, local(): other = lax.ppermute(terms(1 - me).astype(BF16), 'tensor', [(0, 1), (1, 0)])  54 us
    dot_general x24, matrix products, project_back(): return jnp.einsum('lc,dc->ld', grads, weight, preferred_element_type=F32)  53.9 us
    unnamed x353, local copies, waits for them, and re-layouts  52.1 us
    dot_general x20, matrix products, project(): return jnp.dot(inputs, weight, preferred_element_type=F32)  51.3 us
  transfers between devices with their start and end apart: 34, of which 26 were waited for; matrix products, arithmetic and copies ran while one was open for 20% of the time, Pallas kernels for 0%

commit v1 on v0

--- a/solution.py
+++ b/solution.py
@@ -95,7 +95,28 @@
 
 def dp_sum(grads):
     share = lax.psum_scatter(grads, "dp", scatter_dimension=0, tiled=True)
-    return lax.all_gather(share, "dp", axis=0, tiled=True)
+
+    def scan_the_squares(raw, where_dim):
+        across = "dp"
+        n_blocks = lax.axis_size(across)
+        leaves = tuple(((j, (j + 1) % n_blocks) for j in range(n_blocks)))
+        steps_seen = tuple(((j, (j - 1) % n_blocks) for j in range(n_blocks)))
+        passed, r_now = ([raw], [raw])
+        for _ in range(n_blocks // 2):
+            before = lax.ppermute(passed[-1], axis_name=across, perm=leaves)
+            passed.append(before)
+        for _ in range((n_blocks - 1) // 2):
+            response = lax.ppermute(r_now[-1], axis_name=across, perm=steps_seen)
+            r_now.append(response)
+        val2 = jnp.concatenate([*passed[::-1], *r_now[1:]], axis=where_dim)
+        after = jnp.roll(
+            val2,
+            shift=(lax.axis_index(across) - n_blocks // 2) * raw.shape[where_dim],
+            axis=where_dim,
+        )
+        return after
+
+    return scan_the_squares(share, 0)
 
 
 def local(

time: 1480 us -> 1220 us (0.82)
  waiting for transfers between devices: 843 us -> 301 us
  starting transfers between devices: 17.7 us -> 228 us
  local copies, waits for them, and re-layouts: 105 us -> 150 us
    reduce_scatter x10, waiting for transfers between devices: 429 us -> 63.7 us  [dp_sum(): share = lax.psum_scatter(grads, 'dp', scatter_dimension=0, tiled=True)]
    all_gather x10 -> x0, waiting for transfers between devices: 255 us -> none  [dp_sum(): return lax.all_gather(share, 'dp', axis=0, tiled=True)]
    ppermute x0 -> x150, starting transfers between devices: none -> 210 us  [the longest x70 182 us: scan_the_squares(): response = lax.ppermute(r_now[-1], axis_name=across, perm=steps_seen)]
    ppermute x0 -> x150, waiting for transfers between devices: none -> 87.8 us  [the longest x80 80.4 us: scan_the_squares(): before = lax.ppermute(passed[-1], axis_name=across, perm=leaves)]
    unnamed x353 -> x547, local copies, waits for them, and re-layouts: 52.1 us -> 92.7 us
  transfers between devices with their start and end apart: 34 -> 174, of which waited for: 26 -> 48; matrix products, arithmetic and copies ran while one was open for 20% -> 28% of each run, Pallas kernels for 0% -> 0%
where the time goes in v1:
time: 1220 us; the launch traced here: 1200 us
  waiting for transfers between devices  301 us (25%)
  matrix products  294 us (24%)
  starting transfers between devices  228 us (19%)
  local copies, waits for them, and re-layouts  150 us (12%)
  other arithmetic  150 us (12%)
  blocking collectives  62.8 us (5%)
  between operations  17.8 us (1%)
    ppermute x70, starting transfers between devices, scan_the_squares(): response = lax.ppermute(r_now[-1], axis_name=across, perm=steps_seen)  182 us
    ppermute x12, waiting for transfers between devices, tensor_sum(): other = lax.ppermute(mine, 'tensor', [(0, 1), (1, 0)])  99.5 us
    unnamed x547, local copies, waits for them, and re-layouts  92.7 us
    ppermute x80, waiting for transfers between devices, scan_the_squares(): before = lax.ppermute(passed[-1], axis_name=across, perm=leaves)  80.4 us
    reduce_scatter x10, waiting for transfers between devices, dp_sum(): share = lax.psum_scatter(grads, 'dp', scatter_dimension=0, tiled=True)  63.7 us
    psum x1, blocking collectives, local(): summed = lax.psum(jnp.concatenate(vectors), 'dp')  62.8 us
    dot_general x20, matrix products, project(): return jnp.dot(inputs, weight, preferred_element_type=F32)  52.5 us
    ppermute x2, waiting for transfers between devices, local(): other = lax.ppermute(terms(1 - me).astype(BF16), 'tensor', [(0, 1), (1, 0)])  50 us
  transfers between devices with their start and end apart: 174, of which 48 were waited for; matrix products, arithmetic and copies ran while one was open for 28% of the time, Pallas kernels for 0%

profile of v1, /device:TPU:0, one launch (start us, length us, event | category | flops | bytes accessed | tf_op | source)
XLA Modules:
  0.0 1203.9 jit_solution(8123947879602824000)
XLA Ops:
  41.3 9.7 fusion.235
  51.0 8.0 copy_bitcast_fusion
  59.1 4.8 fusion.34
  66.4 4.8 convolution_convert_fusion.3
  81.7 4.7 multiply_reduce_fusion.3
  86.4 5.9 exponential_reduce_fusion.1
  93.8 12.3 %fusion.135 = bf16[8,64,448]{2,1,0:T(8,128)(2,1)} fusion(bf16[1500,8,64]{0,2,1:T(8,128)(2,1)} %bitcast.324, f32[8,448,1500]{2,1,0:T(8,128)} %copy-done.1, f32[8,448]{1,0:T(8,128)S(1)} %log_add_fusion.2), kind=kOutput, calls=%fused_computation.259 | convolution fusion | flops 704485376 | bytes 23513088 | tf_op jit(solution)/shard_map/hlk,khe->lhe/dot_general | solution.py:46
  108.4 21.7 %collective-permute-done.1 = bf16[448,1024]{1,0:T(8,128)(2,1)S(1)} collective-permute-done((bf16[448,1024]{1,0:T(8,128)(2,1)S(1)}, bf16[448,1024]{1,0:T(8,128)(2,1)S(1)}, u32[]{:S(2)}, u32[]{:S(2)}) %collective-permute-start.1) | collective-permute-done | bytes 917536 | tf_op jit(solution)/shard_map/ppermute | solution.py:92
  152.0 15.1 %collective-permute-done.6 = bf16[448,1024]{1,0:T(8,128)(2,1)} collective-permute-done((bf16[448,1024]{1,0:T(8,128)(2,1)}, bf16[448,1024]{1,0:T(8,128)(2,1)}, u32[]{:S(2)}, u32[]{:S(2)}) %collective-permute-start.6) | collective-permute-done | bytes 917536 | tf_op jit(solution)/shard_map/ppermute | solution.py:92
  170.7 13.8 %collective-permute-done.2 = bf16[448,1024]{1,0:T(8,128)(2,1)} collective-permute-done((bf16[448,1024]{1,0:T(8,128)(2,1)}, bf16[448,1024]{1,0:T(8,128)(2,1)}, u32[]{:S(2)}, u32[]{:S(2)}) %collective-permute-start.2) | collective-permute-done | bytes 917536 | tf_op jit(solution)/shard_map/ppermute | solution.py:92
  194.8 15.2 %multiply_reduce_fusion.1 = (f32[8,448]{1,0:T(8,128)S(1)}, f32[8,448,1500]{2,1,0:T(8,128)}) fusion(f32[8,448,1500]{2,1,0:T(8,128)} %copy-done.1, f32[8,448]{1,0:T(8,128)S(1)} %log_add_fusion.2, bf16[448,8,64]{0,2,1:T(8,128)(2,1)} %bitcast.336, bf16[1500,8,64]{0,2,1:T(8,128)(2,1)} %bitcast.325), kind=kOutput, calls=%fused_computation.3 | convolution fusion | flops 709628416 | bytes 45031424 | tf_op jit(solution)/shard_map/lhe,khe->hlk/dot_general | solution.py:55
  209.9 15.0 %multiply_convert_fusion.1 = bf16[8,448,1500]{2,1,0:T(8,128)(2,1)S(1)} fusion(f32[8,448,1500]{2,1,0:T(8,128)} %get-tuple-element.167, f32[8,448,1500]{2,1,0:T(8,128)} %copy-done.1, f32[8,448]{1,0:T(8,128)S(1)} %get-tuple-element.166, f32[8,448]{1,0:T(8,128)S(1)} %log_add_fusion.2), kind=kLoop, calls=%fused_computation.2 | loop fusion | flops 26880000 | bytes 53788672 | tf_op jit(solution)/shard_map/convert_element_type | solution.py:57
  225.0 4.7 convert_reduce_fusion.9
  243.3 5.5 fusion.238
  265.1 9.0 multiply_reduce_fusion.5
  274.8 5.3 multiply_convert_fusion.3
  291.3 5.1 fusion.35
  299.1 5.3 collective-permute-done.3
  316.6 5.7 exponential_reduce_fusion
  324.4 10.5 fusion.138
  338.3 13.3 %convert_reduce_fusion.3 = (f32[8,64]{1,0:T(8,128)}, bf16[8,64,1500]{2,1,0:T(8,128)(2,1)}) fusion(bf16[448,8,64]{0,2,1:T(8,128)(2,1)} %bitcast.337, f32[8,448,1500]{2,1,0:T(8,128)} %copy-done.1, f32[8,448]{1,0:T(8,128)S(1)} %log_add_fusion.2), kind=kOutput, calls=%fused_computation.77 | convolution fusion | flops 706559488 | bytes 23515136 | tf_op jit(solution)/shard_map/hlk,lhe->khe/dot_general | solution.py:64
  374.8 15.9 %collective-permute-done.9 = bf16[448,1024]{1,0:T(8,128)(2,1)S(1)} collective-permute-done((bf16[448,1024]{1,0:T(8,128)(2,1)S(1)}, bf16[448,1024]{1,0:T(8,128)(2,1)S(1)}, u32[]{:S(2)}, u32[]{:S(2)}) %collective-permute-start.9) | collective-permute-done | bytes 917536 | tf_op jit(solution)/shard_map/ppermute | solution.py:92
  392.2 12.4 %collective-permute-done.5 = bf16[448,1024]{1,0:T(8,128)(2,1)S(1)} collective-permute-done((bf16[448,1024]{1,0:T(8,128)(2,1)S(1)}, bf16[448,1024]{1,0:T(8,128)(2,1)S(1)}, u32[]{:S(2)}, u32[]{:S(2)}) %collective-permute-start.5) | collective-permute-done | bytes 917536 | tf_op jit(solution)/shard_map/ppermute | solution.py:92
  413.4 11.7 convert_reduce_fusion.2
  426.4 5.4 fusion.113
  435.8 15.9 %multiply_reduce_fusion = (f32[8,448]{1,0:T(8,128)S(1)}, f32[8,448,1500]{2,1,0:T(8,128)}) fusion(f32[8,448,1500]{2,1,0:T(8,128)} %copy-done.2, f32[8,448]{1,0:T(8,128)S(1)} %log_add_fusion, bf16[448,8,64]{0,2,1:T(8,128)(2,1)} %bitcast.339, bf16[1500,8,64]{0,2,1:T(8,128)(2,1)} %bitcast.322), kind=kOutput, calls=%fused_computation.1 | convolution fusion | flops 709628416 | bytes 45031424 | tf_op jit(solution)/shard_map/lhe,khe->hlk/dot_general | solution.py:55
  451.8 15.0 %multiply_convert_fusion = bf16[8,448,1500]{2,1,0:T(8,128)(2,1)S(1)} fusion(f32[8,448,1500]{2,1,0:T(8,128)} %get-tuple-element.174, f32[8,448,1500]{2,1,0:T(8,128)} %copy-done.2, f32[8,448]{1,0:T(8,128)S(1)} %get-tuple-element.173, f32[8,448]{1,0:T(8,128)S(1)} %log_add_fusion), kind=kLoop, calls=%fused_computation | loop fusion | flops 26880000 | bytes 53788672 | tf_op jit(solution)/shard_map/convert_element_type | solution.py:57
  474.6 5.4 fusion.110
  480.6 8.0 convert_reduce_fusion.8
  492.1 5.8 convert_reduce_fusion.11
  500.7 7.0 collective-permute-done.10
  516.3 5.2 convert_reduce_fusion.10
  532.6 4.7 multiply_reduce_fusion.4
  555.2 8.9 convolution_convert_fusion.1
  576.1 28.9 %collective-permute-done.12 = bf16[1500,512]{1,0:T(8,128)(2,1)S(1)} collective-permute-done((bf16[1500,512]{1,0:T(8,128)(2,1)S(1)}, bf16[1500,512]{1,0:T(8,128)(2,1)S(1)}, u32[]{:S(2)}, u32[]{:S(2)}) %collective-permute-start.12) | collective-permute-done | bytes 1536032 | tf_op jit(solution)/shard_map/ppermute | solution.py:315
  607.7 6.2 convolution_convert_fusion
  627.8 4.6 pad_maximum_fusion.4
  636.5 21.2 %collective-permute-done.13 = bf16[1500,512]{1,0:T(8,128)(2,1)} collective-permute-done((bf16[1500,512]{1,0:T(8,128)(2,1)}, bf16[1500,512]{1,0:T(8,128)(2,1)}, u32[]{:S(2)}, u32[]{:S(2)}) %collective-permute-start.13) | collective-permute-done | bytes 1536032 | tf_op jit(solution)/shard_map/ppermute | solution.py:315
  662.3 12.7 %copy.122 = f32[2,1500,512]{2,0,1:T(2,128)} copy(f32[2,1500,512]{2,1,0:T(8,128)S(1)} %pad_maximum_fusion) | data formatting | bytes 12288000
  707.2 62.8 %psum.7 = f32[13312]{0:T(1024)S(1)} all-reduce(f32[13312]{0:T(1024)} %add_dynamic-update-slice_fusion), channel_id=1, replica_groups=mesh['dp'=16,'tensor'=2] {'dp'}, use_global_device_ids=true, to_apply=%region_64.65 | all-reduce | flops 13312 | bytes 106496 | tf_op jit(solution)/shard_map/psum | solution.py:348
  770.6 5.7 collective-permute-done.109
  776.9 5.9 collective-permute-done.110
  881.1 6.6 collective-permute-done.44
  888.5 6.3 collective-permute-done.45
  896.5 4.6 collective-permute-done.46
  902.9 4.8 collective-permute-done.47
  909.7 4.6 collective-permute-done.48
  1015.1 63.6 %reduce-scatter.29.cloned.1.call-done = bf16[128,1024]{1,0:T(8,128)(2,1)} async-done(((bf16[2048,1024]{1,0:T(8,128)(2,1)}), bf16[128,1024]{1,0:T(8,128)(2,1)}) %reduce-scatter.29.cloned.1.call-update) | async-done | bytes 262160 | tf_op jit(solution)/shard_map/reduce_scatter | solution.py:97
  (1081 shorter events, 630.9 us)
Async XLA Ops:
  7.2 620.6 %reduce-scatter.23.cloned.1.call-start = ((), (), s32[]{:S(2)}) async-start(), calls=%async_computation.16 | async-start | bytes 1114112 | tf_op jit(solution)/shard_map/reduce_scatter | solution.py:97
  38.2 35.6 %collective-permute-start = (bf16[448,1024]{1,0:T(8,128)(2,1)}, bf16[448,1024]{1,0:T(8,128)(2,1)}, u32[]{:S(2)}, u32[]{:S(2)}) collective-permute-start(bf16[448,1024]{1,0:T(8,128)(2,1)} %convolution_convert_fusion.14), channel_id=1, source_target_pairs={{0,1},{1,0},{2,3},{3,2},{4,5},{5,4},{6,7},{7,6},{8,9},{9,8},{10,11... | collective-permute-start | bytes 2752520 | tf_op jit(solution)/shard_map/ppermute | solution.py:92
  108.3 21.9 %collective-permute-start.1 = (bf16[448,1024]{1,0:T(8,128)(2,1)S(1)}, bf16[448,1024]{1,0:T(8,128)(2,1)S(1)}, u32[]{:S(2)}, u32[]{:S(2)}) collective-permute-start(bf16[448,1024]{1,0:T(8,128)(2,1)S(1)} %convolution_convert_fusion.13), channel_id=1, source_target_pairs={{0,1},{1,0},{2,3},{3,2},{4,5},{5,4},{6,7},{7,6},{8,9},{9,8},{10,11... | collective-permute-start | bytes 2752520 | tf_op jit(solution)/shard_map/ppermute | solution.py:92
  143.5 23.5 %collective-permute-start.6 = (bf16[448,1024]{1,0:T(8,128)(2,1)}, bf16[448,1024]{1,0:T(8,128)(2,1)}, u32[]{:S(2)}, u32[]{:S(2)}) collective-permute-start(bf16[448,1024]{1,0:T(8,128)(2,1)} %convolution_convert_fusion.16), channel_id=1, source_target_pairs={{0,1},{1,0},{2,3},{3,2},{4,5},{5,4},{6,7},{7,6},{8,9},{9,8},{10,11... | collective-permute-start | bytes 2752520 | tf_op jit(solution)/shard_map/ppermute | solution.py:92
  146.8 37.6 %collective-permute-start.2 = (bf16[448,1024]{1,0:T(8,128)(2,1)}, bf16[448,1024]{1,0:T(8,128)(2,1)}, u32[]{:S(2)}, u32[]{:S(2)}) collective-permute-start(bf16[448,1024]{1,0:T(8,128)(2,1)} %convolution_convert_fusion.18), channel_id=1, source_target_pairs={{0,1},{1,0},{2,3},{3,2},{4,5},{5,4},{6,7},{7,6},{8,9},{9,8},{10,11... | collective-permute-start | bytes 2752520 | tf_op jit(solution)/shard_map/ppermute | solution.py:92
  232.9 20.4 %collective-permute-start.7 = (bf16[448,1024]{1,0:T(8,128)(2,1)}, bf16[448,1024]{1,0:T(8,128)(2,1)}, u32[]{:S(2)}, u32[]{:S(2)}) collective-permute-start(bf16[448,1024]{1,0:T(8,128)(2,1)} %convolution_convert_fusion.10), channel_id=1, source_target_pairs={{0,1},{1,0},{2,3},{3,2},{4,5},{5,4},{6,7},{7,6},{8,9},{9,8},{10,11... | collective-permute-start | bytes 2752520 | tf_op jit(solution)/shard_map/ppermute | solution.py:92
  284.9 19.5 %collective-permute-start.3 = (bf16[448,1024]{1,0:T(8,128)(2,1)}, bf16[448,1024]{1,0:T(8,128)(2,1)}, u32[]{:S(2)}, u32[]{:S(2)}) collective-permute-start(bf16[448,1024]{1,0:T(8,128)(2,1)} %convolution_convert_fusion.12), channel_id=1, source_target_pairs={{0,1},{1,0},{2,3},{3,2},{4,5},{5,4},{6,7},{7,6},{8,9},{9,8},{10,11... | collective-permute-start | bytes 2752520 | tf_op jit(solution)/shard_map/ppermute | solution.py:92
  367.4 23.3 %collective-permute-start.9 = (bf16[448,1024]{1,0:T(8,128)(2,1)S(1)}, bf16[448,1024]{1,0:T(8,128)(2,1)S(1)}, u32[]{:S(2)}, u32[]{:S(2)}) collective-permute-start(bf16[448,1024]{1,0:T(8,128)(2,1)S(1)} %convolution_convert_fusion.15), channel_id=1, source_target_pairs={{0,1},{1,0},{2,3},{3,2},{4,5},{5,4},{6,7},{7,6},{8,9},{9,8},{10,11... | collective-permute-start | bytes 2752520 | tf_op jit(solution)/shard_map/ppermute | solution.py:92
  371.0 33.6 %collective-permute-start.5 = (bf16[448,1024]{1,0:T(8,128)(2,1)S(1)}, bf16[448,1024]{1,0:T(8,128)(2,1)S(1)}, u32[]{:S(2)}, u32[]{:S(2)}) collective-permute-start(bf16[448,1024]{1,0:T(8,128)(2,1)S(1)} %convolution_convert_fusion.17), channel_id=1, source_target_pairs={{0,1},{1,0},{2,3},{3,2},{4,5},{5,4},{6,7},{7,6},{8,9},{9,8},{10,11... | collective-permute-start | bytes 2752520 | tf_op jit(solution)/shard_map/ppermute | solution.py:92
  431.8 243.3 %reduce-scatter.25.cloned.1.call-start = ((), (), s32[]{:S(2)}) async-start(), calls=%async_computation.17 | async-start | bytes 1114112 | tf_op jit(solution)/shard_map/reduce_scatter | solution.py:97
  451.7 232.6 %reduce-scatter.21.cloned.1.call-start = ((), (), s32[]{:S(2)}) async-start(), calls=%async_computation.15 | async-start | bytes 1114112 | tf_op jit(solution)/shard_map/reduce_scatter | solution.py:97
  480.1 309.4 %reduce-scatter.19.cloned.1.call-start = ((), (), s32[]{:S(2)}) async-start(), calls=%async_computation.14 | async-start | bytes 1114112 | tf_op jit(solution)/shard_map/reduce_scatter | solution.py:97
  500.5 380.5 %reduce-scatter.15.cloned.1.call-start = ((), (), s32[]{:S(2)}) async-start(), calls=%async_computation.12 | async-start | bytes 1114112 | tf_op jit(solution)/shard_map/reduce_scatter | solution.py:97
  524.9 356.2 %reduce-scatter.17.cloned.1.call-start = ((), (), s32[]{:S(2)}) async-start(), calls=%async_computation.13 | async-start | bytes 1114112 | tf_op jit(solution)/shard_map/reduce_scatter | solution.py:97
  532.1 401.8 %reduce-scatter.11.cloned.1.call-start = ((), (), s32[]{:S(2)}) async-start(), calls=%async_computation.10 | async-start | bytes 1114112 | tf_op jit(solution)/shard_map/reduce_scatter | solution.py:97
  547.5 386.4 %reduce-scatter.13.cloned.1.call-start = ((), (), s32[]{:S(2)}) async-start(), calls=%async_computation.11 | async-start | bytes 1114112 | tf_op jit(solution)/shard_map/reduce_scatter | solution.py:97
  555.1 457.9 %reduce-scatter.27.cloned.1.call-start = ((), (), s32[]{:S(2)}) async-start(), calls=%async_computation.18 | async-start | bytes 4456448 | tf_op jit(solution)/shard_map/reduce_scatter | solution.py:97
  564.1 514.6 %reduce-scatter.29.cloned.1.call-start = ((), (), s32[]{:S(2)}) async-start(), calls=%async_computation.19 | async-start | bytes 4456448 | tf_op jit(solution)/shard_map/reduce_scatter | solution.py:97
  568.3 36.6 %collective-permute-start.12 = (bf16[1500,512]{1,0:T(8,128)(2,1)S(1)}, bf16[1500,512]{1,0:T(8,128)(2,1)S(1)}, u32[]{:S(2)}, u32[]{:S(2)}) collective-permute-start(bf16[1500,512]{1,0:T(8,128)(2,1)S(1)} %fusion.36), channel_id=1, source_target_pairs={{0,1},{1,0},{2,3},{3,2},{4,5},{5,4},{6,7},{7,6},{8,9},{9,8},{10,11... | collective-permute-start | bytes 4608008 | tf_op jit(solution)/shard_map/ppermute | solution.py:315
  575.6 104.3 %collective-permute-start.8 = (bf16[448,1024]{1,0:T(8,128)(2,1)}, bf16[448,1024]{1,0:T(8,128)(2,1)}, u32[]{:S(2)}, u32[]{:S(2)}) collective-permute-start(bf16[448,1024]{1,0:T(8,128)(2,1)} %add_convert_fusion.1), channel_id=1, source_target_pairs={{0,1},{1,0},{2,3},{3,2},{4,5},{5,4},{6,7},{7,6},{8,9},{9,8},{10,11... | collective-permute-start | bytes 2752520 | tf_op jit(solution)/shard_map/ppermute | solution.py:92
  619.1 38.6 %collective-permute-start.13 = (bf16[1500,512]{1,0:T(8,128)(2,1)}, bf16[1500,512]{1,0:T(8,128)(2,1)}, u32[]{:S(2)}, u32[]{:S(2)}) collective-permute-start(bf16[1500,512]{1,0:T(8,128)(2,1)} %fusion.37), channel_id=1, source_target_pairs={{0,1},{1,0},{2,3},{3,2},{4,5},{5,4},{6,7},{7,6},{8,9},{9,8},{10,11... | collective-permute-start | bytes 4608008 | tf_op jit(solution)/shard_map/ppermute | solution.py:315
  627.5 57.0 %collective-permute-start.11 = (bf16[448,1024]{1,0:T(8,128)(2,1)}, bf16[448,1024]{1,0:T(8,128)(2,1)}, u32[]{:S(2)}, u32[]{:S(2)}) collective-permute-start(bf16[448,1024]{1,0:T(8,128)(2,1)} %add_convert_fusion), channel_id=1, source_target_pairs={{0,1},{1,0},{2,3},{3,2},{4,5},{5,4},{6,7},{7,6},{8,9},{9,8},{10,11... | collective-permute-start | bytes 2752520 | tf_op jit(solution)/shard_map/ppermute | solution.py:92
  635.0 26.3 %collective-permute-start.105 = (bf16[64,512]{1,0:T(8,128)(2,1)S(1)}, bf16[64,512]{1,0:T(8,128)(2,1)S(1)}, u32[]{:S(2)}, u32[]{:S(2)}) collective-permute-start(bf16[64,512]{1,0:T(8,128)(2,1)S(1)} %collective-permute-done.104), channel_id=1, source_target_pairs={{0,2},{2,4},{4,6},{6,8},{8,10},{10,12},{12,14},{14,16},{16,18},{18... | collective-permute-start | bytes 196616 | tf_op jit(solution)/shard_map/ppermute | solution.py:106
  661.3 23.1 %collective-permute-start.106 = (bf16[64,512]{1,0:T(8,128)(2,1)S(1)}, bf16[64,512]{1,0:T(8,128)(2,1)S(1)}, u32[]{:S(2)}, u32[]{:S(2)}) collective-permute-start(bf16[64,512]{1,0:T(8,128)(2,1)S(1)} %collective-permute-done.105), channel_id=1, source_target_pairs={{0,2},{2,4},{4,6},{6,8},{8,10},{10,12},{12,14},{14,16},{16,18},{18... | collective-permute-start | bytes 196616 | tf_op jit(solution)/shard_map/ppermute | solution.py:106
  675.1 114.4 %collective-permute-start.127 = (bf16[32,1024]{1,0:T(8,128)(2,1)}, bf16[32,1024]{1,0:T(8,128)(2,1)S(1)}, u32[]{:S(2)}, u32[]{:S(2)}) collective-permute-start(bf16[32,1024]{1,0:T(8,128)(2,1)} %reduce-scatter.25.cloned.1.call-done), channel_id=1, source_target_pairs={{0,30},{2,0},{4,2},{6,4},{8,6},{10,8},{12,10},{14,12},{16,14},{18,... | collective-permute-start | bytes 196616 | tf_op jit(solution)/shard_map/ppermute | solution.py:109
  679.5 114.5 %collective-permute-start.119 = (bf16[32,1024]{1,0:T(8,128)(2,1)}, bf16[32,1024]{1,0:T(8,128)(2,1)S(1)}, u32[]{:S(2)}, u32[]{:S(2)}) collective-permute-start(bf16[32,1024]{1,0:T(8,128)(2,1)} %reduce-scatter.25.cloned.1.call-done), channel_id=1, source_target_pairs={{0,2},{2,4},{4,6},{6,8},{8,10},{10,12},{12,14},{14,16},{16,18},{18... | collective-permute-start | bytes 196616 | tf_op jit(solution)/shard_map/ppermute | solution.py:106
  680.0 114.0 %collective-permute-start.112 = (bf16[64,512]{1,0:T(8,128)(2,1)S(1)}, bf16[64,512]{1,0:T(8,128)(2,1)S(1)}, u32[]{:S(2)}, u32[]{:S(2)}) collective-permute-start(bf16[64,512]{1,0:T(8,128)(2,1)S(1)} %copy-done.110), channel_id=1, source_target_pairs={{0,30},{2,0},{4,2},{6,4},{8,6},{10,8},{12,10},{14,12},{16,14},{18,... | collective-permute-start | bytes 196616 | tf_op jit(solution)/shard_map/ppermute | solution.py:109
  684.4 114.1 %collective-permute-start.97 = (bf16[64,512]{1,0:T(8,128)(2,1)}, bf16[64,512]{1,0:T(8,128)(2,1)S(1)}, u32[]{:S(2)}, u32[]{:S(2)}) collective-permute-start(bf16[64,512]{1,0:T(8,128)(2,1)} %reduce-scatter.21.cloned.1.call-done), channel_id=1, source_target_pairs={{0,30},{2,0},{4,2},{6,4},{8,6},{10,8},{12,10},{14,12},{16,14},{18,... | collective-permute-start | bytes 196616 | tf_op jit(solution)/shard_map/ppermute | solution.py:109
  702.1 67.8 %collective-permute-start.108 = (bf16[64,512]{1,0:T(8,128)(2,1)S(1)}, bf16[64,512]{1,0:T(8,128)(2,1)S(1)}, u32[]{:S(2)}, u32[]{:S(2)}) collective-permute-start(bf16[64,512]{1,0:T(8,128)(2,1)S(1)} %collective-permute-done.107), channel_id=1, source_target_pairs={{0,2},{2,4},{4,6},{6,8},{8,10},{10,12},{12,14},{14,16},{16,18},{18... | collective-permute-start | bytes 196616 | tf_op jit(solution)/shard_map/ppermute | solution.py:106
  865.3 55.4 %collective-permute-start.133 = (bf16[32,1024]{1,0:T(8,128)(2,1)S(1)}, bf16[32,1024]{1,0:T(8,128)(2,1)S(1)}, u32[]{:S(2)}, u32[]{:S(2)}) collective-permute-start(bf16[32,1024]{1,0:T(8,128)(2,1)S(1)} %collective-permute-done.132), channel_id=1, source_target_pairs={{0,30},{2,0},{4,2},{6,4},{8,6},{10,8},{12,10},{14,12},{16,14},{18,... | collective-permute-start | bytes 196616 | tf_op jit(solution)/shard_map/ppermute | solution.py:109
  929.5 24.9 %collective-permute-start.52 = (bf16[64,512]{1,0:T(8,128)(2,1)S(1)}, bf16[64,512]{1,0:T(8,128)(2,1)}, u32[]{:S(2)}, u32[]{:S(2)}) collective-permute-start(bf16[64,512]{1,0:T(8,128)(2,1)S(1)} %copy-done.105), channel_id=1, source_target_pairs={{0,30},{2,0},{4,2},{6,4},{8,6},{10,8},{12,10},{14,12},{16,14},{18,... | collective-permute-start | bytes 196616 | tf_op jit(solution)/shard_map/ppermute | solution.py:109
  940.5 19.2 %collective-permute-start.22 = (bf16[64,512]{1,0:T(8,128)(2,1)}, bf16[64,512]{1,0:T(8,128)(2,1)S(1)}, u32[]{:S(2)}, u32[]{:S(2)}) collective-permute-start(bf16[64,512]{1,0:T(8,128)(2,1)} %reduce-scatter.11.cloned.1.call-done), channel_id=1, source_target_pairs={{0,30},{2,0},{4,2},{6,4},{8,6},{10,8},{12,10},{14,12},{16,14},{18,... | collective-permute-start | bytes 196616 | tf_op jit(solution)/shard_map/ppermute | solution.py:109
  984.9 98.5 %collective-permute-start.55 = (bf16[64,512]{1,0:T(8,128)(2,1)}, bf16[64,512]{1,0:T(8,128)(2,1)}, u32[]{:S(2)}, u32[]{:S(2)}) collective-permute-start(bf16[64,512]{1,0:T(8,128)(2,1)} %collective-permute-done.54), channel_id=1, source_target_pairs={{0,30},{2,0},{4,2},{6,4},{8,6},{10,8},{12,10},{14,12},{16,14},{18,... | collective-permute-start | bytes 196616 | tf_op jit(solution)/shard_map/ppermute | solution.py:109
  989.3 98.0 %collective-permute-start.25 = (bf16[64,512]{1,0:T(8,128)(2,1)}, bf16[64,512]{1,0:T(8,128)(2,1)}, u32[]{:S(2)}, u32[]{:S(2)}) collective-permute-start(bf16[64,512]{1,0:T(8,128)(2,1)} %collective-permute-done.24), channel_id=1, source_target_pairs={{0,30},{2,0},{4,2},{6,4},{8,6},{10,8},{12,10},{14,12},{16,14},{18,... | collective-permute-start | bytes 196616 | tf_op jit(solution)/shard_map/ppermute | solution.py:109
  989.4 101.8 %collective-permute-start.40 = (bf16[64,512]{1,0:T(8,128)(2,1)}, bf16[64,512]{1,0:T(8,128)(2,1)}, u32[]{:S(2)}, u32[]{:S(2)}) collective-permute-start(bf16[64,512]{1,0:T(8,128)(2,1)} %collective-permute-done.39), channel_id=1, source_target_pairs={{0,30},{2,0},{4,2},{6,4},{8,6},{10,8},{12,10},{14,12},{16,14},{18,... | collective-permute-start | bytes 196616 | tf_op jit(solution)/shard_map/ppermute | solution.py:109
  1013.0 65.7 %collective-permute-start.134 = (bf16[64,2048]{1,0:T(8,128)(2,1)}, bf16[64,2048]{1,0:T(8,128)(2,1)}, u32[]{:S(2)}, u32[]{:S(2)}) collective-permute-start(bf16[64,2048]{1,0:T(8,128)(2,1)} %reduce-scatter.27.cloned.1.call-done), channel_id=1, source_target_pairs={{0,2},{2,4},{4,6},{6,8},{8,10},{10,12},{12,14},{14,16},{16,18},{18... | collective-permute-start | bytes 786440 | tf_op jit(solution)/shard_map/ppermute | solution.py:106
  1083.4 25.4 %collective-permute-start.142 = (bf16[64,2048]{1,0:T(8,128)(2,1)S(1)}, bf16[64,2048]{1,0:T(8,128)(2,1)S(1)}, u32[]{:S(2)}, u32[]{:S(2)}) collective-permute-start(bf16[64,2048]{1,0:T(8,128)(2,1)S(1)} %copy-done.73), channel_id=1, source_target_pairs={{0,30},{2,0},{4,2},{6,4},{8,6},{10,8},{12,10},{14,12},{16,14},{18,... | collective-permute-start | bytes 786440 | tf_op jit(solution)/shard_map/ppermute | solution.py:109
  1087.4 21.5 %collective-permute-start.157 = (bf16[128,1024]{1,0:T(8,128)(2,1)S(1)}, bf16[128,1024]{1,0:T(8,128)(2,1)S(1)}, u32[]{:S(2)}, u32[]{:S(2)}) collective-permute-start(bf16[128,1024]{1,0:T(8,128)(2,1)S(1)} %copy-done.74), channel_id=1, source_target_pairs={{0,30},{2,0},{4,2},{6,4},{8,6},{10,8},{12,10},{14,12},{16,14},{18,... | collective-permute-start | bytes 786440 | tf_op jit(solution)/shard_map/ppermute | solution.py:109
  1087.8 21.1 %collective-permute-start.150 = (bf16[128,1024]{1,0:T(8,128)(2,1)S(1)}, bf16[128,1024]{1,0:T(8,128)(2,1)S(1)}, u32[]{:S(2)}, u32[]{:S(2)}) collective-permute-start(bf16[128,1024]{1,0:T(8,128)(2,1)S(1)} %collective-permute-done.149), channel_id=1, source_target_pairs={{0,2},{2,4},{4,6},{6,8},{8,10},{10,12},{12,14},{14,16},{16,18},{18... | collective-permute-start | bytes 786440 | tf_op jit(solution)/shard_map/ppermute | solution.py:106
  1108.8 19.5 %collective-permute-start.143 = (bf16[64,2048]{1,0:T(8,128)(2,1)S(1)}, bf16[64,2048]{1,0:T(8,128)(2,1)S(1)}, u32[]{:S(2)}, u32[]{:S(2)}) collective-permute-start(bf16[64,2048]{1,0:T(8,128)(2,1)S(1)} %collective-permute-done.142), channel_id=1, source_target_pairs={{0,30},{2,0},{4,2},{6,4},{8,6},{10,8},{12,10},{14,12},{16,14},{18,... | collective-permute-start | bytes 786440 | tf_op jit(solution)/shard_map/ppermute | solution.py:109
  1108.9 19.5 %collective-permute-start.158 = (bf16[128,1024]{1,0:T(8,128)(2,1)S(1)}, bf16[128,1024]{1,0:T(8,128)(2,1)S(1)}, u32[]{:S(2)}, u32[]{:S(2)}) collective-permute-start(bf16[128,1024]{1,0:T(8,128)(2,1)S(1)} %collective-permute-done.157), channel_id=1, source_target_pairs={{0,30},{2,0},{4,2},{6,4},{8,6},{10,8},{12,10},{14,12},{16,14},{18,... | collective-permute-start | bytes 786440 | tf_op jit(solution)/shard_map/ppermute | solution.py:109
  1108.9 19.5 %collective-permute-start.151 = (bf16[128,1024]{1,0:T(8,128)(2,1)S(1)}, bf16[128,1024]{1,0:T(8,128)(2,1)S(1)}, u32[]{:S(2)}, u32[]{:S(2)}) collective-permute-start(bf16[128,1024]{1,0:T(8,128)(2,1)S(1)} %collective-permute-done.150), channel_id=1, source_target_pairs={{0,2},{2,4},{4,6},{6,8},{8,10},{10,12},{12,14},{14,16},{16,18},{18... | collective-permute-start | bytes 786440 | tf_op jit(solution)/shard_map/ppermute | solution.py:106
  1109.4 19.5 %collective-permute-start.137 = (bf16[64,2048]{1,0:T(8,128)(2,1)S(1)}, bf16[64,2048]{1,0:T(8,128)(2,1)S(1)}, u32[]{:S(2)}, u32[]{:S(2)}) collective-permute-start(bf16[64,2048]{1,0:T(8,128)(2,1)S(1)} %collective-permute-done.136), channel_id=1, source_target_pairs={{0,2},{2,4},{4,6},{6,8},{8,10},{10,12},{12,14},{14,16},{16,18},{18... | collective-permute-start | bytes 786440 | tf_op jit(solution)/shard_map/ppermute | solution.py:106
  1128.3 19.3 %collective-permute-start.144 = (bf16[64,2048]{1,0:T(8,128)(2,1)S(1)}, bf16[64,2048]{1,0:T(8,128)(2,1)S(1)}, u32[]{:S(2)}, u32[]{:S(2)}) collective-permute-start(bf16[64,2048]{1,0:T(8,128)(2,1)S(1)} %collective-permute-done.143), channel_id=1, source_target_pairs={{0,30},{2,0},{4,2},{6,4},{8,6},{10,8},{12,10},{14,12},{16,14},{18,... | collective-permute-start | bytes 786440 | tf_op jit(solution)/shard_map/ppermute | solution.py:109
  1128.4 19.3 %collective-permute-start.159 = (bf16[128,1024]{1,0:T(8,128)(2,1)S(1)}, bf16[128,1024]{1,0:T(8,128)(2,1)S(1)}, u32[]{:S(2)}, u32[]{:S(2)}) collective-permute-start(bf16[128,1024]{1,0:T(8,128)(2,1)S(1)} %collective-permute-done.158), channel_id=1, source_target_pairs={{0,30},{2,0},{4,2},{6,4},{8,6},{10,8},{12,10},{14,12},{16,14},{18,... | collective-permute-start | bytes 786440 | tf_op jit(solution)/shard_map/ppermute | solution.py:109
  1128.4 19.3 %collective-permute-start.152 = (bf16[128,1024]{1,0:T(8,128)(2,1)S(1)}, bf16[128,1024]{1,0:T(8,128)(2,1)S(1)}, u32[]{:S(2)}, u32[]{:S(2)}) collective-permute-start(bf16[128,1024]{1,0:T(8,128)(2,1)S(1)} %collective-permute-done.151), channel_id=1, source_target_pairs={{0,2},{2,4},{4,6},{6,8},{8,10},{10,12},{12,14},{14,16},{16,18},{18... | collective-permute-start | bytes 786440 | tf_op jit(solution)/shard_map/ppermute | solution.py:106
  1128.9 19.3 %collective-permute-start.138 = (bf16[64,2048]{1,0:T(8,128)(2,1)S(1)}, bf16[64,2048]{1,0:T(8,128)(2,1)S(1)}, u32[]{:S(2)}, u32[]{:S(2)}) collective-permute-start(bf16[64,2048]{1,0:T(8,128)(2,1)S(1)} %collective-permute-done.137), channel_id=1, source_target_pairs={{0,2},{2,4},{4,6},{6,8},{8,10},{10,12},{12,14},{14,16},{16,18},{18... | collective-permute-start | bytes 786440 | tf_op jit(solution)/shard_map/ppermute | solution.py:106
  1143.1 29.8 %collective-permute-start.43 = (bf16[64,512]{1,0:T(8,128)(2,1)S(1)}, bf16[64,512]{1,0:T(8,128)(2,1)S(1)}, u32[]{:S(2)}, u32[]{:S(2)}) collective-permute-start(bf16[64,512]{1,0:T(8,128)(2,1)S(1)} %collective-permute-done.42), channel_id=1, source_target_pairs={{0,30},{2,0},{4,2},{6,4},{8,6},{10,8},{12,10},{14,12},{16,14},{18,... | collective-permute-start | bytes 196616 | tf_op jit(solution)/shard_map/ppermute | solution.py:109
  (306 other events, 3041.7 us)
Sparse Core Ops, SparseCore 0:
  431.9 58.0 reduce-scatter.22
  493.6 56.6 reduce-scatter.24
  554.0 56.6 reduce-scatter.20
  614.1 56.5 reduce-scatter.18
  674.2 56.8 reduce-scatter.14
  734.5 57.2 reduce-scatter.16
  795.5 58.2 reduce-scatter.10
  857.4 58.4 reduce-scatter.12
  920.4 81.6 reduce-scatter.26
  1006.3 72.3 reduce-scatter.28
